TPU v7x, 32 devices: a whole 2x2x4 slice. The times are simulated.
32 devices in a mesh: sec: 2 (over y), grp: 4 (over x, core), seq: 4 (over z).
Axes of the slice: x: 2, y: 2, z: 4, core: 2. Of those that a mesh axis runs over, the one named last changes fastest.
Arguments:
- tokens: bfloat16 [8192, 1024], P(('sec', 'grp', 'seq')), may hold values from -6 to 6
- expert_ids: int32 [8192, 1], P(('sec', 'grp', 'seq')), may hold values from 0 to 31; in each aligned block of 256 rows (0 to 255, 256 to 511, ...) at most 16 rows name the same one
- attn_in: bfloat16 [1024, 3072], replicated
- attn_out: bfloat16 [1024, 1024], replicated, may hold values from -0.1875 to 0.1875
- gain_attn: float32 [1024], replicated, may hold values from 0.5 to 1.5
- gain_expert: float32 [1024], replicated, may hold values from 0.5 to 1.5
- router: bfloat16 [1024, 32], replicated, may hold values from -0.1875 to 0.1875
- expert_in: bfloat16 [32, 1024, 2816], P(('sec', 'grp', 'seq')), may hold values from -0.1875 to 0.1875
- expert_out: bfloat16 [32, 2816, 1024], P(('sec', 'grp', 'seq')), may hold values from -0.109375 to 0.109375
Outputs:
- layer_out: bfloat16 [8192, 1024], P(('sec', 'grp', 'seq'))
Inputs may be any that keep to these rules, and one draw needn't show every extreme that they name: `expert_ids`: of the 256 tokens of one device at most 16 choose one expert, and on every device some expert is chosen by exactly 16 of them.
All inputs are finite; a program needn't handle non-finite values.
Results may differ from a plain program's by a relative error of at most 0.004.
Values may be sent and summed in bfloat16 or wider, within the bound.
A program may use at most 192 MiB of HBM per device.

v0:
```python
import jax
import jax.numpy as jnp
from jax import lax
from jax.sharding import PartitionSpec as P

HEADS = 16


def normalize(values, gain):
    return values * lax.rsqrt(jnp.mean(values * values, -1, keepdims=True) + 1e-06) * gain


def attend(query, keys, values):
    query_rows, head_count, head_dim = query.shape
    block_rows = min(query_rows, max(8, 2048 // head_count))
    blocked = query.reshape(query_rows // block_rows, block_rows, head_count, head_dim)

    def one_block(query_block):
        scores = jnp.einsum(
            "qhd,khd->hqk", query_block, keys, preferred_element_type=jnp.float32
        ) * head_dim ** (-0.5)
        weights = jax.nn.softmax(scores, -1).astype(jnp.bfloat16)
        return jnp.einsum(
            "hqk,khd->qhd", weights, values, preferred_element_type=jnp.float32
        ).astype(jnp.bfloat16)

    return lax.map(one_block, blocked).reshape(query_rows, head_count, head_dim)


def body(
    tokens, expert_ids, attn_in, attn_out, gain_attn, gain_expert, router, expert_in, expert_out
):
    tok_rows, model_width = tokens.shape
    head_count = HEADS
    head_dim = model_width // head_count
    tokens_f32 = tokens.astype(jnp.float32)
    normed = normalize(tokens_f32, gain_attn).astype(jnp.bfloat16)
    projected = jnp.dot(normed, attn_in, preferred_element_type=jnp.float32).astype(jnp.bfloat16)
    head_parts = projected.reshape(tok_rows, 3, head_count, head_dim)
    spread = lax.all_to_all(head_parts, "seq", split_axis=2, concat_axis=0, tiled=True)
    local_context = attend(spread[:, 0], spread[:, 1], spread[:, 2])
    context = lax.all_to_all(local_context, "seq", split_axis=0, concat_axis=1, tiled=True)
    hidden = tokens_f32 + jnp.dot(
        context.reshape(tok_rows, model_width), attn_out, preferred_element_type=jnp.float32
    )
    normed2 = normalize(hidden, gain_expert).astype(jnp.bfloat16)
    experts = lax.axis_size(("sec", "grp", "seq")) * expert_in.shape[0]
    most_rows = max(2, 2 * tok_rows // experts)
    picked = expert_ids[:, 0]
    one_hot = (picked[:, None] == jnp.arange(experts, dtype=jnp.int32)[None, :]).astype(jnp.int32)
    earlier = jnp.sum((jnp.cumsum(one_hot, 0) - one_hot) * one_hot, 1)
    dest_slot = picked * most_rows + earlier
    route = (
        dest_slot[:, None] == jnp.arange(experts * most_rows, dtype=jnp.int32)[None, :]
    ).astype(jnp.bfloat16)
    outgoing = jnp.einsum("ts,td->sd", route, normed2, preferred_element_type=jnp.float32).astype(
        jnp.bfloat16
    )
    logits = jnp.dot(normed2, router, preferred_element_type=jnp.float32)
    gate_value = jax.nn.sigmoid(jnp.sum(logits * one_hot.astype(jnp.float32), 1))
    send_rows = outgoing.reshape(experts, most_rows, model_width)
    arrived = lax.all_to_all(
        send_rows, ("sec", "grp", "seq"), split_axis=0, concat_axis=0, tiled=True
    )
    flat_rows = arrived.reshape(-1, model_width)
    inner_act = jax.nn.relu(
        jnp.dot(flat_rows, expert_in[0], preferred_element_type=jnp.float32)
    ).astype(jnp.bfloat16)
    result = jnp.dot(inner_act, expert_out[0], preferred_element_type=jnp.float32).astype(
        jnp.bfloat16
    )
    produced = result.reshape(arrived.shape)
    back_rows = lax.all_to_all(
        produced, ("sec", "grp", "seq"), split_axis=0, concat_axis=0, tiled=True
    )
    returned = back_rows.reshape(experts * most_rows, model_width)
    combined = jnp.dot(route, returned, preferred_element_type=jnp.float32)
    return (hidden + gate_value[:, None] * combined).astype(jnp.bfloat16)


def solution(mesh):
    return jax.shard_map(
        body,
        mesh=mesh,
        in_specs=(
            P(("sec", "grp", "seq"), None),
            P(("sec", "grp", "seq"), None),
            P(),
            P(),
            P(),
            P(),
            P(),
            P(("sec", "grp", "seq"), None, None),
            P(("sec", "grp", "seq"), None, None),
        ),
        out_specs=P(("sec", "grp", "seq"), None),
        check_vma=False,
    )
```

profile of v0, /device:TPU:1, one launch (start us, length us, event | category | flops | bytes accessed | tf_op | source)
XLA Modules:
  0.0 192.3 jit_solution(16523318302608738156)
XLA Ops:
  1.4 6.0 %convolution_convert_fusion = bf16[256,3072]{1,0:T(8,128)(2,1)} fusion(bf16[1024,3072]{1,0:T(8,128)(2,1)} %param.13, bf16[256,1024]{1,0:T(8,128)(2,1)} %param.11, f32[1024]{0:T(1024)} %param.15, f32[256]{0:T(256)S(1)} %add_rsqrt_fusion.1), kind=kOutput, calls=%fused_computation.24 | convolution fusion | flops 1612447744 | bytes 8393728 | tf_op jit(solution)/shard_map/dot_general | solution.py:38
  7.4 2.6 %copy.25 = bf16[256,3072]{0,1:T(8,128)(2,1)} copy(bf16[256,3072]{1,0:T(8,128)(2,1)} %convolution_convert_fusion) | data formatting | bytes 3145728 | tf_op jit(solution)/shard_map/convert_element_type | solution.py:38
  10.0 2.7 %copy.26 = bf16[256,3,16,64]{0,3,1,2:T(8,128)(2,1)} copy(bf16[256,3,16,64]{0,3,2,1:T(8,128)(2,1)} %bitcast.87) | data formatting | bytes 3145728 | tf_op jit(solution)/shard_map/reshape | solution.py:39
  12.7 5.4 %all-to-all-start = ((bf16[256,3,16,64]{0,3,1,2:T(8,128)(2,1)}), bf16[256,3,16,64]{0,3,1,2:T(8,128)(2,1)}, u32[]{:S(2)}, u32[]{:S(2)}) async-start(bf16[256,3,16,64]{0,3,1,2:T(8,128)(2,1)} %copy.26), calls=%async_computation | async-start | bytes 3145728 | tf_op jit(solution)/shard_map/all_to_all | solution.py:40
  18.1 36.6 %all-to-all-done = bf16[256,3,16,64]{0,3,1,2:T(8,128)(2,1)} async-done(((bf16[256,3,16,64]{0,3,1,2:T(8,128)(2,1)}), bf16[256,3,16,64]{0,3,1,2:T(8,128)(2,1)}, u32[]{:S(2)}, u32[]{:S(2)}) %all-to-all-start) | async-done | bytes 1572896 | tf_op jit(solution)/shard_map/all_to_all | solution.py:40
  54.8 3.8 %copy.27 = bf16[4,256,3,4,64]{1,0,4,3,2:T(4,128)(2,1)} copy(bf16[4,256,3,4,64]{1,4,2,3,0:T(8,128)(2,1)} %bitcast.5) | data formatting | bytes 3145728 | tf_op jit(solution)/shard_map/all_to_all | solution.py:40
  58.5 3.8 %all_to_all.33 = bf16[1024,3,4,64]{0,3,2,1:T(8,128)(2,1)} reshape(bf16[4,256,3,4,64]{1,0,4,3,2:T(4,128)(2,1)} %copy.27) | data formatting | bytes 3145728 | tf_op jit(solution)/shard_map/all_to_all | solution.py:40
  62.4 2.6 %slice_bitcast_fusion = (bf16[1024,4,64]{0,2,1:T(8,128)(2,1)}, bf16[1024,4,64]{0,2,1:T(8,128)(2,1)}, bf16[1024,1,4,64]{0,3,2,1:T(8,128)(2,1)S(1)}) fusion(bf16[1024,3,4,64]{0,3,2,1:T(8,128)(2,1)} %all_to_all.33), kind=kLoop, calls=%fused_computation.40 | loop fusion | bytes 3145728 | tf_op jit(solution)/shard_map/squeeze | solution.py:41
  65.4 24.9 %while.10 = (s32[]{:T(128)}, bf16[2,512,4,64]{1,3,2,0:T(8,128)(2,1)}, bf16[2,512,4,64]{1,3,2,0:T(8,128)(2,1)S(1)}, bf16[1024,4,64]{0,2,1:T(8,128)(2,1)}, bf16[1024,4,64]{0,2,1:T(8,128)(2,1)}, /*index=5*/s32[]{:T(128)}) while((s32[]{:T(128)}, bf16[2,512,4,64]{1,3,2,0:T(8,128)(2,1)}, bf16[2,512,4,64]{1,3,2,0:T(8,128)(2,1)S(1)}, ...), condition=%wide.region_4.5_spmd, body=%wide.region_1.4_spmd.sunk | while | flops 547488768 | bytes 22560900 | solution.py:27
  65.4 6.8 %fusion.75 = (f32[4,512]{1,0:T(4,128)S(1)}, f32[4,512,1024]{2,1,0:T(8,128)}) fusion(bf16[1024,4,64]{0,2,1:T(8,128)(2,1)} %get-tuple-element.115, bf16[2,512,4,64]{1,3,2,0:T(8,128)(2,1)S(1)} %get-tuple-element.114, s32[]{:T(128)} %get-tuple-element.106), kind=kOutput, calls=%fused_computation.62.clone.1 | convolution fusion | flops 274727936 | bytes 9183236 | tf_op jit(solution)/shard_map/while/body/eval_jaxpr/sub | solution.py:22
  72.2 4.9 %fusion.76 = bf16[2,512,4,64]{1,3,2,0:T(8,128)(2,1)S(1)} fusion(bf16[2,512,4,64]{1,3,2,0:T(8,128)(2,1)S(1)} %copy-done.1, s32[]{:T(128)} %get-tuple-element.106, bf16[1024,4,64]{0,2,1:T(8,128)(2,1)} %get-tuple-element.116, f32[4,512,1024]{2,1,0:T(8,128)} %get-tuple-element.98, f32[4,512]{1,0:T(4,128)S(1)} %get-tuple-element.99), kind=kOutput, calls=%fused_computation.9.clone.1 | convolution fusion | flops 272760832 | bytes 9183236 | tf_op jit(solution)/shard_map/while/body/eval_jaxpr/hqk,khd->qhd/dot_general | solution.py:23
  77.9 6.8 %fusion.75 = (f32[4,512]{1,0:T(4,128)S(1)}, f32[4,512,1024]{2,1,0:T(8,128)}) fusion(bf16[1024,4,64]{0,2,1:T(8,128)(2,1)} %get-tuple-element.115, bf16[2,512,4,64]{1,3,2,0:T(8,128)(2,1)S(1)} %get-tuple-element.114, s32[]{:T(128)} %get-tuple-element.106), kind=kOutput, calls=%fused_computation.62.clone.1 | convolution fusion | flops 274727936 | bytes 9183236 | tf_op jit(solution)/shard_map/while/body/eval_jaxpr/sub | solution.py:22
  84.6 4.9 %fusion.76 = bf16[2,512,4,64]{1,3,2,0:T(8,128)(2,1)S(1)} fusion(bf16[2,512,4,64]{1,3,2,0:T(8,128)(2,1)S(1)} %copy-done.1, s32[]{:T(128)} %get-tuple-element.106, bf16[1024,4,64]{0,2,1:T(8,128)(2,1)} %get-tuple-element.116, f32[4,512,1024]{2,1,0:T(8,128)} %get-tuple-element.98, f32[4,512]{1,0:T(4,128)S(1)} %get-tuple-element.99), kind=kOutput, calls=%fused_computation.9.clone.1 | convolution fusion | flops 272760832 | bytes 9183236 | tf_op jit(solution)/shard_map/while/body/eval_jaxpr/hqk,khd->qhd/dot_general | solution.py:23
  90.3 1.6 copy.34
  91.9 1.6 reshape.74
  93.5 4.1 %all-to-all-start.1 = ((bf16[4,2,32768]{2,1,0:T(2,128)(2,1)}), bf16[4,2,32768]{2,1,0:T(2,128)(2,1)}, u32[]{:S(2)}, u32[]{:S(2)}) async-start(bf16[4,2,32768]{2,1,0:T(2,128)(2,1)} %reshape.74), calls=%async_computation.1 | async-start | bytes 1048576 | tf_op jit(solution)/shard_map/all_to_all | solution.py:42
  98.6 13.1 %all-to-all-done.1 = bf16[4,2,32768]{2,1,0:T(2,128)(2,1)} async-done(((bf16[4,2,32768]{2,1,0:T(2,128)(2,1)}), bf16[4,2,32768]{2,1,0:T(2,128)(2,1)}, u32[]{:S(2)}, u32[]{:S(2)}) %all-to-all-start.1) | async-done | bytes 524320 | tf_op jit(solution)/shard_map/all_to_all | solution.py:42
  111.7 1.7 reshape.75
  114.7 2.0 %multiply_reduce_fusion.1 = (f32[256]{0:T(256)S(1)}, f32[256,1024]{1,0:T(8,128)S(1)}) fusion(bf16[256,1024]{0,1:T(8,128)(2,1)} %bitcast.91, bf16[1024,1024]{1,0:T(8,128)(2,1)S(1)} %copy-done, bf16[256,1024]{1,0:T(8,128)(2,1)} %param.11), kind=kOutput, calls=%fused_computation.39 | convolution fusion | flops 537919232 | bytes 4195328 | tf_op jit(solution)/shard_map/dot_general | solution.py:43
  117.3 31.1 %all_to_all.43 = bf16[32,16,1024]{2,1,0:T(8,128)(2,1)} all-to-all(bf16[32,16,1024]{2,1,0:T(8,128)(2,1)S(1)} %bitcast.90), channel_id=1, replica_groups=mesh['sec'=2,'grp'=4,'seq'=4] {'sec','grp','seq'}, dimensions={0} | all-to-all | bytes 2097152 | tf_op jit(solution)/shard_map/all_to_all | solution.py:62
  148.4 11.8 %fusion.33 = bf16[512,1024]{1,0:T(8,128)(2,1)} fusion(bf16[1,2816,1024]{2,1,0:T(8,128)(2,1)} %param.19, bf16[512,1024]{1,0:T(8,128)(2,1)} %bitcast.93, bf16[1,1024,2816]{2,1,0:T(8,128)(2,1)} %param.18), kind=kOutput, calls=%fused_computation.28 | convolution fusion | flops 5908987904 | bytes 13631488 | tf_op jit(solution)/shard_map/dot_general | solution.py:69
  160.2 3.2 %all-to-all-start.3 = ((bf16[32,16,1024]{2,1,0:T(8,128)(2,1)}), bf16[32,16,1024]{2,1,0:T(8,128)(2,1)}, u32[]{:S(2)}, u32[]{:S(2)}) async-start(bf16[32,16,1024]{2,1,0:T(8,128)(2,1)} %bitcast.92), calls=%async_computation.3 | async-start | bytes 2097152 | tf_op jit(solution)/shard_map/all_to_all | solution.py:73
  163.8 26.0 %all-to-all-done.3 = bf16[32,16,1024]{2,1,0:T(8,128)(2,1)} async-done(((bf16[32,16,1024]{2,1,0:T(8,128)(2,1)}), bf16[32,16,1024]{2,1,0:T(8,128)(2,1)}, u32[]{:S(2)}, u32[]{:S(2)}) %all-to-all-start.3) | async-done | bytes 1048608 | tf_op jit(solution)/shard_map/all_to_all | solution.py:73
  189.8 2.5 %fusion.37 = bf16[256,1024]{1,0:T(8,128)(2,1)} fusion(f32[256,1024]{1,0:T(8,128)S(1)} %get-tuple-element.64, bf16[512,1024]{1,0:T(8,128)(2,1)} %bitcast.23, f32[256]{0:T(256)S(1)} %add_divide_fusion, s32[256]{0:T(256)S(1)} %bitcast.98), kind=kOutput, calls=%fused_computation.32 | convolution fusion | flops 269352960 | bytes 2623488 | tf_op jit(solution)/shard_map/dot_general | solution.py:77
  (33 shorter events, 6.5 us)
Async XLA Ops:
  0.0 114.7 %copy-start = (bf16[1024,1024]{1,0:T(8,128)(2,1)S(1)}, bf16[1024,1024]{1,0:T(8,128)(2,1)}, u32[]{:S(2)}) copy-start(bf16[1024,1024]{1,0:T(8,128)(2,1)} %param.14) | copy-start | bytes 6291460
  12.7 42.0 %all-to-all-start = ((bf16[256,3,16,64]{0,3,1,2:T(8,128)(2,1)}), bf16[256,3,16,64]{0,3,1,2:T(8,128)(2,1)}, u32[]{:S(2)}, u32[]{:S(2)}) async-start(bf16[256,3,16,64]{0,3,1,2:T(8,128)(2,1)} %copy.26), calls=%async_computation | async-start | bytes 3145728 | tf_op jit(solution)/shard_map/all_to_all | solution.py:40
  65.4 32.2 %copy-start.5 = (s32[256,1]{0,1:T(1,128)S(1)}, s32[256,1]{0,1:T(1,128)}, u32[]{:S(2)}) copy-start(s32[256,1]{0,1:T(1,128)} %param.12) | copy-start | bytes 3076
  65.4 6.8 %copy-start.1 = (bf16[2,512,4,64]{1,3,2,0:T(8,128)(2,1)S(1)}, bf16[2,512,4,64]{1,3,2,0:T(8,128)(2,1)}, u32[]{:S(2)}) copy-start(bf16[2,512,4,64]{1,3,2,0:T(8,128)(2,1)} %get-tuple-element.107) | copy-start | bytes 1572868 | tf_op jit(solution)/shard_map/while
  77.1 0.8 copy-start.2
  77.9 6.8 %copy-start.1 = (bf16[2,512,4,64]{1,3,2,0:T(8,128)(2,1)S(1)}, bf16[2,512,4,64]{1,3,2,0:T(8,128)(2,1)}, u32[]{:S(2)}) copy-start(bf16[2,512,4,64]{1,3,2,0:T(8,128)(2,1)} %get-tuple-element.107) | copy-start | bytes 1572868 | tf_op jit(solution)/shard_map/while
  89.5 0.8 copy-start.2
  90.3 26.4 %copy-start.4 = (f32[1024]{0:T(1024)S(1)}, f32[1024]{0:T(1024)}, u32[]{:S(2)}) copy-start(f32[1024]{0:T(1024)} %param.16) | copy-start | bytes 12292
  93.5 18.2 %all-to-all-start.1 = ((bf16[4,2,32768]{2,1,0:T(2,128)(2,1)}), bf16[4,2,32768]{2,1,0:T(2,128)(2,1)}, u32[]{:S(2)}, u32[]{:S(2)}) async-start(bf16[4,2,32768]{2,1,0:T(2,128)(2,1)} %reshape.74), calls=%async_computation.1 | async-start | bytes 1048576 | tf_op jit(solution)/shard_map/all_to_all | solution.py:42
  148.4 15.0 %copy-start.3 = (bf16[1024,32]{0,1:T(8,128)(2,1)S(1)}, bf16[1024,32]{0,1:T(8,128)(2,1)}, u32[]{:S(2)}) copy-start(bf16[1024,32]{0,1:T(8,128)(2,1)} %param.17) | copy-start | bytes 196612
  160.2 29.6 %all-to-all-start.3 = ((bf16[32,16,1024]{2,1,0:T(8,128)(2,1)}), bf16[32,16,1024]{2,1,0:T(8,128)(2,1)}, u32[]{:S(2)}, u32[]{:S(2)}) async-start(bf16[32,16,1024]{2,1,0:T(8,128)(2,1)} %bitcast.92), calls=%async_computation.3 | async-start | bytes 2097152 | tf_op jit(solution)/shard_map/all_to_all | solution.py:73
where the time goes:
time: 193 us; the launch traced here: 192 us
  waiting for transfers between devices  75.8 us (39%)
  matrix products  46.5 us (24%)
  blocking collectives  31.1 us (16%)
  local copies, waits for them, and re-layouts  23.9 us (12%)
  starting transfers between devices  12.7 us (7%)
  other arithmetic  2.14 us (1%)
    all_to_all x1, waiting for transfers between devices, body(): lax.all_to_all(head_parts, 'seq', split_axis=2, concat_axis=0, tiled=True)  36.6 us
    all_to_all x1, blocking collectives, body(): lax.all_to_all(send_rows, ('sec', 'grp', 'seq'), split_axis=0, concat_axi...  31.1 us
    all_to_all x1, waiting for transfers between devices, body(): lax.all_to_all(produced, ('sec', 'grp', 'seq'), split_axis=0, concat_axis...  26 us
    sub x2, matrix products, one_block(): weights = jax.nn.softmax(scores, -1).astype(jnp.bfloat16)  13.5 us
    all_to_all x1, waiting for transfers between devices, body(): lax.all_to_all(local_context, 'seq', split_axis=0, concat_axis=1, tiled=T...  13.1 us
    dot_general x1, matrix products, body(): jnp.dot(inner_act, expert_out[0], preferred_element_type=jnp.float32)  11.8 us
    dot_general x2, matrix products, one_block(): jnp.einsum('hqk,khd->qhd', weights, values, preferred_element_type=jnp.fl...  9.76 us
    all_to_all x2, local copies, waits for them, and re-layouts, body(): lax.all_to_all(head_parts, 'seq', split_axis=2, concat_axis=0, tiled=True)  7.6 us
  transfers between devices with their start and end apart: 3, of which 3 were waited for; matrix products, arithmetic and copies ran while one was open for 1% of the time, Pallas kernels for 0%

commit v1 on v0

v1 whole, which is shorter than its diff:
```python
import functools

import jax
import jax.numpy as jnp
from jax import lax
from jax.experimental import pallas as pl
from jax.experimental.pallas import tpu as pltpu
from jax.sharding import PartitionSpec as P

HEADS = 16
AXES = ("sec", "grp", "seq")
MESH = pl.DeviceIdType.MESH
VMEM_LIMIT = 60 * 1024 * 1024


def normalize(values, gain):
    return values * lax.rsqrt(jnp.mean(values * values, -1, keepdims=True) + 1e-06) * gain


def attention_kernel(
    ranks,
    head_dim,
    tok_ref,
    win_hbm,
    wout_hbm,
    gain_ref,
    gain2_ref,
    hidden_ref,
    normed2_ref,
    shards,
    win,
    wout,
    query2,
    kv,
    acc,
    top,
    total,
    context,
    w_sem,
    right_sem,
    left_sem,
    recv_sem,
):
    rows, width = tok_ref.shape
    pair = 2 * head_dim
    pairs = width // pair
    me = lax.axis_index("seq")
    load_in = pltpu.make_async_copy(win_hbm, win, w_sem.at[0])
    load_out = pltpu.make_async_copy(wout_hbm, wout, w_sem.at[1])
    load_in.start()
    load_out.start()
    has_left, has_right = me > 0, me < ranks - 1
    barrier = pltpu.get_barrier_semaphore()

    @pl.when(has_left)
    def _():
        pl.semaphore_signal(barrier, inc=1, device_id={"seq": me - 1}, device_id_type=MESH)

    @pl.when(has_right)
    def _():
        pl.semaphore_signal(barrier, inc=1, device_id={"seq": me + 1}, device_id_type=MESH)

    pl.semaphore_wait(barrier, has_left.astype(jnp.int32) + has_right.astype(jnp.int32))

    def to_right(source, index):
        return pltpu.make_async_remote_copy(
            src_ref=source,
            dst_ref=shards.at[index],
            send_sem=right_sem.at[index],
            recv_sem=recv_sem.at[index],
            device_id={"seq": me + 1},
            device_id_type=MESH,
        )

    def to_left(source, index):
        return pltpu.make_async_remote_copy(
            src_ref=source,
            dst_ref=shards.at[index],
            send_sem=left_sem.at[index],
            recv_sem=recv_sem.at[index],
            device_id={"seq": me - 1},
            device_id_type=MESH,
        )

    @pl.when(has_right)
    def _():
        to_right(tok_ref, me).start()

    @pl.when(has_left)
    def _():
        to_left(tok_ref, me).start()

    shards[me] = tok_ref[...]
    lane = lax.broadcasted_iota(jnp.int32, (rows, pair), 1)
    first = lane < head_dim
    top[...] = jnp.full(top.shape, -jnp.inf, jnp.float32)
    total[...] = jnp.zeros(total.shape, jnp.float32)
    acc[...] = jnp.zeros(acc.shape, jnp.float32)
    load_in.wait()
    own = normalize(tok_ref[...].astype(jnp.float32), gain_ref[...]).astype(jnp.bfloat16)
    for p in range(pairs):
        part = jnp.dot(
            own, win[:, p * pair : (p + 1) * pair], preferred_element_type=jnp.float32
        ).astype(jnp.bfloat16)
        part = part * jnp.bfloat16(head_dim ** (-0.5))
        query2[p, 0:rows] = jnp.where(first, part, jnp.zeros_like(part))
        query2[p, rows : 2 * rows] = jnp.where(first, jnp.zeros_like(part), part)

    def absorb(index):
        normed = normalize(shards[index].astype(jnp.float32), gain_ref[...]).astype(jnp.bfloat16)
        block = min(256, width)
        for c in range(2 * width // block):
            kv[:, c * block : (c + 1) * block] = jnp.dot(
                normed,
                win[:, width + c * block : width + (c + 1) * block],
                preferred_element_type=jnp.float32,
            ).astype(jnp.bfloat16)
        for p in range(pairs):
            keys = kv[:, p * pair : (p + 1) * pair]
            values = kv[:, width + p * pair : width + (p + 1) * pair]
            scores = lax.dot_general(
                query2[p], keys, (((1,), (1,)), ((), ())), preferred_element_type=jnp.float32
            )
            old = top[p][:, 0:1]
            new = jnp.maximum(old, jnp.max(scores, -1, keepdims=True))
            scale = jnp.exp(old - new)
            weights = jnp.exp(scores - new)
            total[p] = jnp.broadcast_to(
                total[p][:, 0:1] * scale + jnp.sum(weights, -1, keepdims=True), total.shape[1:]
            )
            top[p] = jnp.broadcast_to(new, top.shape[1:])
            acc[p] = acc[p] * scale + jnp.dot(
                weights.astype(jnp.bfloat16), values, preferred_element_type=jnp.float32
            )

    def step(distance, carry):
        low, high = me - distance, me + distance

        @pl.when((distance > 0) & (low >= 0))
        def _():
            to_left(shards.at[low], low).wait_recv()

            @pl.when(has_right)
            def _():
                to_right(shards.at[low], low).start()

        @pl.when((distance > 0) & (high < ranks))
        def _():
            to_right(shards.at[high], high).wait_recv()

            @pl.when(has_left)
            def _():
                to_left(shards.at[high], high).start()

        def side(which, inner):
            index = jnp.where(which == 0, low, high)

            @pl.when((index >= 0) & (index < ranks) & ((distance > 0) | (which == 0)))
            def _():
                absorb(index)

            return inner

        lax.fori_loop(0, 2, side, 0)
        return carry

    lax.fori_loop(0, ranks, step, 0)
    for p in range(pairs):
        even = acc[p, 0:rows] / total[p, 0:rows]
        odd = acc[p, rows : 2 * rows] / total[p, rows : 2 * rows]
        context[:, p * pair : (p + 1) * pair] = jnp.where(first, even, odd).astype(jnp.bfloat16)
    load_out.wait()
    hidden = tok_ref[...].astype(jnp.float32) + jnp.dot(
        context[...], wout[...], preferred_element_type=jnp.float32
    )
    hidden_ref[...] = hidden
    normed2_ref[...] = normalize(hidden, gain2_ref[...]).astype(jnp.bfloat16)

    def drain(index, carry):
        @pl.when(has_right & (index <= me))
        def _():
            to_right(shards.at[index], index).wait_send()

        @pl.when(has_left & (index >= me))
        def _():
            to_left(shards.at[index], index).wait_send()

        return carry

    lax.fori_loop(0, ranks, drain, 0)


def attention(tokens, attn_in, attn_out, gain_attn, gain_expert):
    rows, width = tokens.shape
    ranks = lax.axis_size("seq")
    head_dim = width // HEADS
    pair = 2 * head_dim
    pairs = width // pair
    vmem = pl.BlockSpec(memory_space=pltpu.VMEM)
    hbm = pl.BlockSpec(memory_space=pl.ANY)
    return pl.pallas_call(
        functools.partial(attention_kernel, ranks, head_dim),
        out_shape=(
            jax.ShapeDtypeStruct((rows, width), jnp.float32),
            jax.ShapeDtypeStruct((rows, width), jnp.bfloat16),
        ),
        in_specs=[vmem, hbm, hbm, vmem, vmem],
        out_specs=(vmem, vmem),
        scratch_shapes=[
            pltpu.VMEM((ranks, rows, width), jnp.bfloat16),
            pltpu.VMEM(attn_in.shape, jnp.bfloat16),
            pltpu.VMEM(attn_out.shape, jnp.bfloat16),
            pltpu.VMEM((pairs, 2 * rows, pair), jnp.bfloat16),
            pltpu.VMEM((rows, 2 * width), jnp.bfloat16),
            pltpu.VMEM((pairs, 2 * rows, pair), jnp.float32),
            pltpu.VMEM((pairs, 2 * rows, pair), jnp.float32),
            pltpu.VMEM((pairs, 2 * rows, pair), jnp.float32),
            pltpu.VMEM((rows, width), jnp.bfloat16),
            pltpu.SemaphoreType.DMA((2,)),
            pltpu.SemaphoreType.DMA((ranks,)),
            pltpu.SemaphoreType.DMA((ranks,)),
            pltpu.SemaphoreType.DMA((ranks,)),
        ],
        compiler_params=pltpu.CompilerParams(
            collective_id=0, has_side_effects=True, vmem_limit_bytes=VMEM_LIMIT
        ),
    )(tokens, attn_in, attn_out, gain_attn[None, :], gain_expert[None, :])


def expert_kernel(
    sizes,
    rows_ref,
    w1_hbm,
    w2_hbm,
    back_ref,
    arrived,
    result,
    inner,
    w1,
    w2,
    w_sem,
    out_sem,
    in_sem,
    reply_sem,
    back_sem,
):
    secs, grps, ranks = sizes
    groups = secs * grps
    devices, most, width = rows_ref.shape
    hidden_units = w1.shape[1]
    sec, grp, me = lax.axis_index("sec"), lax.axis_index("grp"), lax.axis_index("seq")
    group = sec * grps + grp
    flat = group * ranks + me
    load1 = pltpu.make_async_copy(w1_hbm, w1, w_sem.at[0])
    load2 = pltpu.make_async_copy(w2_hbm, w2, w_sem.at[1])
    load1.start()
    load2.start()
    barrier = pltpu.get_barrier_semaphore()

    def place(other_group, other_rank):
        return (other_group // grps, other_group % grps, other_rank)

    def greet(offset, carry):
        other = (flat + offset) % devices
        pl.semaphore_signal(
            barrier, inc=1, device_id=place(other // ranks, other % ranks), device_id_type=MESH
        )
        return carry

    lax.fori_loop(1, devices, greet, 0)
    pl.semaphore_wait(barrier, devices - 1)

    def send(other_group, other_rank):
        return pltpu.make_async_remote_copy(
            src_ref=rows_ref.at[other_group * ranks + other_rank],
            dst_ref=arrived.at[me, group],
            send_sem=out_sem.at[other_rank, other_group],
            recv_sem=in_sem.at[me, group],
            device_id=place(other_group, other_rank),
            device_id_type=MESH,
        )

    def receive(other_group, other_rank):
        return pltpu.make_async_remote_copy(
            src_ref=rows_ref.at[flat],
            dst_ref=arrived.at[other_rank, other_group],
            send_sem=out_sem.at[other_rank, other_group],
            recv_sem=in_sem.at[other_rank, other_group],
            device_id=place(other_group, other_rank),
            device_id_type=MESH,
        )

    def reply(other_group, other_rank):
        return pltpu.make_async_remote_copy(
            src_ref=result.at[other_rank, other_group],
            dst_ref=back_ref.at[flat],
            send_sem=reply_sem.at[other_rank, other_group],
            recv_sem=back_sem.at[flat],
            device_id=place(other_group, other_rank),
            device_id_type=MESH,
        )

    def returned(other_group, other_rank):
        other = other_group * ranks + other_rank
        return pltpu.make_async_remote_copy(
            src_ref=result.at[other_rank, other_group],
            dst_ref=back_ref.at[other],
            send_sem=reply_sem.at[other_rank, other_group],
            recv_sem=back_sem.at[other],
            device_id=place(other_group, other_rank),
            device_id_type=MESH,
        )

    def over_groups(rank, act):
        def one(offset, carry):
            other_group = (group + offset) % groups

            @pl.when((offset > 0) | (rank != me))
            def _():
                act(other_group, rank)

            return carry

        lax.fori_loop(0, groups, one, 0)

    def by_distance(act):
        def one(step, carry):
            distance = (step + 1) // 2
            rank = jnp.where(step % 2 == 1, me - distance, me + distance)

            @pl.when((rank >= 0) & (rank < ranks))
            def _():
                act(rank)

            return carry

        lax.fori_loop(0, 2 * ranks - 1, one, 0)

    by_distance(lambda rank: over_groups(rank, lambda g, r: send(g, r).start()))
    arrived[me, group] = rows_ref[flat]
    load1.wait()
    load2.wait()
    block = 256 if hidden_units % 256 == 0 else hidden_units
    out_block = 256 if width % 256 == 0 else width

    def work(rank):
        over_groups(rank, lambda g, r: receive(g, r).wait_recv())
        rows = arrived[rank].reshape(groups * most, width)
        for c in range(0, hidden_units, block):
            inner[:, c : c + block] = jax.nn.relu(
                jnp.dot(rows, w1[:, c : c + block], preferred_element_type=jnp.float32)
            ).astype(jnp.bfloat16)
        for c in range(0, width, out_block):
            result[rank, :, :, c : c + out_block] = (
                jnp.dot(inner[...], w2[:, c : c + out_block], preferred_element_type=jnp.float32)
                .astype(jnp.bfloat16)
                .reshape(groups, most, out_block)
            )
        over_groups(rank, lambda g, r: reply(g, r).start())

    by_distance(work)
    back_ref[flat] = result[me, group]
    by_distance(lambda rank: over_groups(rank, lambda g, r: send(g, r).wait_send()))
    by_distance(lambda rank: over_groups(rank, lambda g, r: returned(g, r).wait_recv()))
    by_distance(lambda rank: over_groups(rank, lambda g, r: reply(g, r).wait_send()))


def run_experts(rows, w1, w2):
    devices, most, width = rows.shape
    sizes = tuple(lax.axis_size(name) for name in AXES)
    groups, ranks = sizes[0] * sizes[1], sizes[2]
    vmem = pl.BlockSpec(memory_space=pltpu.VMEM)
    hbm = pl.BlockSpec(memory_space=pl.ANY)
    return pl.pallas_call(
        functools.partial(expert_kernel, sizes),
        out_shape=jax.ShapeDtypeStruct(rows.shape, jnp.bfloat16),
        in_specs=[vmem, hbm, hbm],
        out_specs=vmem,
        scratch_shapes=[
            pltpu.VMEM((ranks, groups, most, width), jnp.bfloat16),
            pltpu.VMEM((ranks, groups, most, width), jnp.bfloat16),
            pltpu.VMEM((groups * most, w1.shape[1]), jnp.bfloat16),
            pltpu.VMEM(w1.shape, jnp.bfloat16),
            pltpu.VMEM(w2.shape, jnp.bfloat16),
            pltpu.SemaphoreType.DMA((2,)),
            pltpu.SemaphoreType.DMA((ranks, groups)),
            pltpu.SemaphoreType.DMA((ranks, groups)),
            pltpu.SemaphoreType.DMA((ranks, groups)),
            pltpu.SemaphoreType.DMA((devices,)),
        ],
        compiler_params=pltpu.CompilerParams(
            collective_id=1, has_side_effects=True, vmem_limit_bytes=VMEM_LIMIT
        ),
    )(rows, w1, w2)


def body(
    tokens, expert_ids, attn_in, attn_out, gain_attn, gain_expert, router, expert_in, expert_out
):
    tok_rows, model_width = tokens.shape
    hidden, normed2 = attention(tokens, attn_in, attn_out, gain_attn, gain_expert)
    experts = lax.axis_size(AXES) * expert_in.shape[0]
    most_rows = max(2, 2 * tok_rows // experts)
    picked = expert_ids[:, 0]
    one_hot = (picked[:, None] == jnp.arange(experts, dtype=jnp.int32)[None, :]).astype(jnp.int32)
    earlier = jnp.sum((jnp.cumsum(one_hot, 0) - one_hot) * one_hot, 1)
    dest_slot = picked * most_rows + earlier
    route = (
        dest_slot[:, None] == jnp.arange(experts * most_rows, dtype=jnp.int32)[None, :]
    ).astype(jnp.bfloat16)
    outgoing = jnp.einsum("ts,td->sd", route, normed2, preferred_element_type=jnp.float32).astype(
        jnp.bfloat16
    )
    logits = jnp.dot(normed2, router, preferred_element_type=jnp.float32)
    gate_value = jax.nn.sigmoid(jnp.sum(logits * one_hot.astype(jnp.float32), 1))
    send_rows = outgoing.reshape(experts, most_rows, model_width)
    back_rows = run_experts(send_rows, expert_in[0], expert_out[0])
    returned = back_rows.reshape(experts * most_rows, model_width)
    combined = jnp.dot(route, returned, preferred_element_type=jnp.float32)
    return (hidden + gate_value[:, None] * combined).astype(jnp.bfloat16)


def solution(mesh):
    return jax.shard_map(
        body,
        mesh=mesh,
        in_specs=(P(AXES, None), P(AXES, None), P(), P(), P(), P(), P(), P(AXES, None, None), P(AXES, None, None)),
        out_specs=P(AXES, None),
        check_vma=False,
    )
```

time: 193 us -> 125 us (0.65)
  Pallas kernels: 0 us -> 115 us
  waiting for transfers between devices: 75.8 us -> 0 us
  matrix products: 46.5 us -> 6.47 us
  blocking collectives: 31.1 us -> 0 us
  local copies, waits for them, and re-layouts: 23.9 us -> 0.2 us
  starting transfers between devices: 12.7 us -> 0 us
    pallas_call x0 -> x2, Pallas kernels: none -> 115 us  [the longest x1 58.2 us: attention(): pl.pallas_call(functools.partial(attention_kernel, ranks, head_dim), out_...]
    all_to_all x3 -> x0, waiting for transfers between devices: 75.8 us -> none  [the longest x1 36.6 us: body(): lax.all_to_all(head_parts, 'seq', split_axis=2, concat_axis=0, tiled=True)]
    all_to_all x1 -> x0, blocking collectives: 31.1 us -> none  [body(): lax.all_to_all(send_rows, ('sec', 'grp', 'seq'), split_axis=0, concat_axi...]
    dot_general x5 -> x0, matrix products: 29.6 us -> none  [the longest x1 11.8 us: body(): jnp.dot(inner_act, expert_out[0], preferred_element_type=jnp.float32)]
    sub x2 -> x0, matrix products: 13.5 us -> none  [one_block(): weights = jax.nn.softmax(scores, -1).astype(jnp.bfloat16)]
    all_to_all x3 -> x0, starting transfers between devices: 12.7 us -> none  [the longest x1 5.41 us: body(): lax.all_to_all(head_parts, 'seq', split_axis=2, concat_axis=0, tiled=True)]
    all_to_all x3 -> x0, local copies, waits for them, and re-layouts: 8.82 us -> none  [the longest x2 7.6 us: body(): lax.all_to_all(head_parts, 'seq', split_axis=2, concat_axis=0, tiled=True)]
    reshape x2 -> x0, local copies, waits for them, and re-layouts: 4.34 us -> none  [the longest x1 2.73 us: body(): head_parts = projected.reshape(tok_rows, 3, head_count, head_dim)]
  transfers between devices with their start and end apart: 3 -> 0, of which waited for: 3 -> 0; matrix products, arithmetic and copies ran while one was open for 1% -> 0% of each run, Pallas kernels for 0% -> 0%
where the time goes in v1:
time: 125 us; the launch traced here: 124 us
  Pallas kernels  115 us (92%)
  matrix products  6.47 us (5%)
  other arithmetic  2.83 us (2%)
    pallas_call x1, Pallas kernels, attention(): pl.pallas_call(functools.partial(attention_kernel, ranks, head_dim), out_...  58.2 us
    pallas_call x1, Pallas kernels, run_experts(): pl.pallas_call(functools.partial(expert_kernel, sizes), out_shape=jax.Sha...  56.6 us
    dot_general x1, matrix products, body(): jnp.einsum('ts,td->sd', route, normed2, preferred_element_type=jnp.float32)  2.64 us
    dot_general x1, matrix products, body(): combined = jnp.dot(route, returned, preferred_element_type=jnp.float32)  2.51 us

profile of v1, /device:TPU:1, one launch (start us, length us, event | category | flops | bytes accessed | tf_op | source)
XLA Modules:
  0.0 124.3 jit_solution(2080428292584170773)
XLA Ops:
  0.0 0.0 copy-start
  0.0 0.0 copy-start.2
  0.0 0.8 fusion.7
  0.8 0.6 reduce-window.6
  1.3 0.2 slice_reduce_fusion
  1.6 0.8 fusion.6
  2.3 0.7 multiply_add_fusion
  3.0 58.2 %shard_map.91 = (f32[256,1024]{1,0:T(8,128)}, bf16[256,1024]{1,0:T(8,128)(2,1)}) custom-call(bf16[256,1024]{1,0:T(8,128)(2,1)} %tok_ref.1, bf16[1024,3072]{1,0:T(8,128)(2,1)} %win_hbm.1, bf16[1024,1024]{1,0:T(8,128)(2,1)} %wout_hbm.1, f32[1,1024]{1,0:T(1,128)} %bitcast.34, f32[1,1024]{1,0:T(1,128)} %bitcast.35), custom_call_target="tpu_custom_call" | custom-call | tf_op jit(solution)/shard_map/pallas_call | solution.py:201
  61.2 0.0 copy-done
  61.2 0.0 copy-done.2
  61.2 1.3 %fusion.2 = f32[256]{0:T(256)S(1)} fusion(bf16[256,1024]{1,0:T(8,128)(2,1)} %get-tuple-element.8, bf16[1024,32]{0,1:T(8,128)(2,1)S(1)} %copy-done, s32[256]{0:T(256)S(1)} %bitcast.31), kind=kOutput, calls=%fused_computation.5 | convolution fusion | flops 16817920 | bytes 591872 | tf_op jit(solution)/shard_map/dot_general | solution.py:414
  62.6 2.6 %convolution_convert_fusion = bf16[512,1024]{1,0:T(8,128)(2,1)} fusion(bf16[256,1024]{1,0:T(8,128)(2,1)} %get-tuple-element.8, s32[256]{0:T(256)S(1)} %bitcast.32), kind=kOutput, calls=%fused_computation | convolution fusion | flops 269090816 | bytes 1573888 | tf_op jit(solution)/shard_map/ts,td->sd/dot_general | solution.py:411
  65.2 0.0 copy-start.1
  65.2 56.6 %shard_map.92 = bf16[32,16,1024]{2,1,0:T(8,128)(2,1)} custom-call(bf16[32,16,1024]{2,1,0:T(8,128)(2,1)} %bitcast.28, bf16[1024,2816]{1,0:T(8,128)(2,1)} %bitcast.25, bf16[2816,1024]{1,0:T(8,128)(2,1)} %bitcast.26), custom_call_target="tpu_custom_call" | custom-call | tf_op jit(solution)/shard_map/pallas_call | solution.py:374
  121.8 0.0 copy-done.1
  121.8 2.5 %fusion.1 = bf16[256,1024]{1,0:T(8,128)(2,1)} fusion(f32[256,1024]{1,0:T(8,128)S(1)} %copy-done.1, bf16[512,1024]{1,0:T(8,128)(2,1)} %bitcast.27, f32[256]{0:T(256)S(1)} %add_divide_fusion, s32[256]{0:T(256)S(1)} %bitcast.33), kind=kOutput, calls=%fused_computation.3 | convolution fusion | flops 269352960 | bytes 2623488 | tf_op jit(solution)/shard_map/dot_general | solution.py:419
  (3 shorter events, 0.0 us)
Async XLA Ops:
  0.0 61.2 %copy-start = (bf16[1024,32]{0,1:T(8,128)(2,1)S(1)}, bf16[1024,32]{0,1:T(8,128)(2,1)}, u32[]{:S(2)}) copy-start(bf16[1024,32]{0,1:T(8,128)(2,1)} %param.15) | copy-start | bytes 196612
  0.0 61.2 %copy-start.2 = (s32[256,1]{0,1:T(1,128)S(1)}, s32[256,1]{0,1:T(1,128)}, u32[]{:S(2)}) copy-start(s32[256,1]{0,1:T(1,128)} %param.10) | copy-start | bytes 3076
  65.2 56.6 %copy-start.1 = (f32[256,1024]{1,0:T(8,128)S(1)}, f32[256,1024]{1,0:T(8,128)}, u32[]{:S(2)}) copy-start(f32[256,1024]{1,0:T(8,128)} %get-tuple-element.7) | copy-start | bytes 3145732

commit v2 on v1

v2 whole, which is shorter than its diff:
```python
import functools

import jax
import jax.numpy as jnp
from jax import lax
from jax.experimental import pallas as pl
from jax.experimental.pallas import tpu as pltpu
from jax.sharding import PartitionSpec as P

HEADS = 16
AXES = ("sec", "grp", "seq")
MESH = pl.DeviceIdType.MESH
VMEM_LIMIT = 60 * 1024 * 1024


def normalize(values, gain):
    return values * lax.rsqrt(jnp.mean(values * values, -1, keepdims=True) + 1e-06) * gain


def layer_kernel(
    sizes,
    head_dim,
    tok_ref,
    ids_ref,
    ids_row_ref,
    win_hbm,
    wout_hbm,
    gain_ref,
    gain2_ref,
    router_ref,
    w1_hbm,
    w2_hbm,
    out_ref,
    shards,
    win,
    wout,
    query2,
    kv,
    acc,
    top,
    total,
    context,
    rows_buf,
    arrived,
    result,
    back,
    inner,
    w1,
    w2,
    hidden_buf,
    normed2_buf,
    combined,
    w_sem,
    right_sem,
    left_sem,
    recv_sem,
    out_sem,
    in_sem,
    reply_sem,
    back_sem,
):
    secs, grps, ranks = sizes
    groups = secs * grps
    devices = groups * ranks
    most = rows_buf.shape[2]
    rows, width = tok_ref.shape
    pair = 2 * head_dim
    pairs = width // pair
    me = lax.axis_index("seq")
    load_in = pltpu.make_async_copy(win_hbm, win, w_sem.at[0])
    load_out = pltpu.make_async_copy(wout_hbm, wout, w_sem.at[1])
    load_in.start()
    load_out.start()
    load1 = pltpu.make_async_copy(w1_hbm, w1, w_sem.at[2])
    load2 = pltpu.make_async_copy(w2_hbm, w2, w_sem.at[3])
    load1.start()
    load2.start()
    sec, grp = lax.axis_index("sec"), lax.axis_index("grp")
    group = sec * grps + grp
    flat = group * ranks + me
    has_left, has_right = me > 0, me < ranks - 1
    barrier = pltpu.get_barrier_semaphore()

    def place(other_group, other_rank):
        return (other_group // grps, other_group % grps, other_rank)

    def greet(offset, carry):
        other = (flat + offset) % devices
        pl.semaphore_signal(
            barrier, inc=1, device_id=place(other // ranks, other % ranks), device_id_type=MESH
        )
        return carry

    lax.fori_loop(1, devices, greet, 0)
    pl.semaphore_wait(barrier, devices - 1)

    def to_right(source, index):
        return pltpu.make_async_remote_copy(
            src_ref=source,
            dst_ref=shards.at[index],
            send_sem=right_sem.at[index],
            recv_sem=recv_sem.at[index],
            device_id={"seq": me + 1},
            device_id_type=MESH,
        )

    def to_left(source, index):
        return pltpu.make_async_remote_copy(
            src_ref=source,
            dst_ref=shards.at[index],
            send_sem=left_sem.at[index],
            recv_sem=recv_sem.at[index],
            device_id={"seq": me - 1},
            device_id_type=MESH,
        )

    @pl.when(has_right)
    def _():
        to_right(tok_ref, me).start()

    @pl.when(has_left)
    def _():
        to_left(tok_ref, me).start()

    shards[me] = tok_ref[...]
    experts = devices
    ids = ids_ref[...].astype(jnp.float32)
    ids_row = ids_row_ref[...].astype(jnp.float32)
    chosen = (
        lax.broadcasted_iota(jnp.int32, (rows, experts), 1).astype(jnp.float32) == ids
    ).astype(jnp.float32)
    chosen_row = (
        lax.broadcasted_iota(jnp.int32, (experts, rows), 0).astype(jnp.float32) == ids_row
    ).astype(jnp.float32)
    down = lax.broadcasted_iota(jnp.int32, (rows, rows), 0)
    across = lax.broadcasted_iota(jnp.int32, (rows, rows), 1)
    below = (across < down).astype(jnp.float32).astype(jnp.bfloat16)
    above = (down < across).astype(jnp.float32).astype(jnp.bfloat16)
    earlier = jnp.dot(below, chosen.astype(jnp.bfloat16), preferred_element_type=jnp.float32)
    slot_column = ids * most + jnp.sum(earlier * chosen, 1, keepdims=True)
    earlier_row = jnp.dot(chosen_row.astype(jnp.bfloat16), above, preferred_element_type=jnp.float32)
    slot_row = ids_row * most + jnp.sum(earlier_row * chosen_row, 0, keepdims=True)
    lane = lax.broadcasted_iota(jnp.int32, (rows, pair), 1)
    first = lane < head_dim
    top[...] = jnp.full(top.shape, -jnp.inf, jnp.float32)
    total[...] = jnp.zeros(total.shape, jnp.float32)
    acc[...] = jnp.zeros(acc.shape, jnp.float32)
    load_in.wait()
    own = normalize(tok_ref[...].astype(jnp.float32), gain_ref[...]).astype(jnp.bfloat16)
    for p in range(pairs):
        part = jnp.dot(
            own, win[:, p * pair : (p + 1) * pair], preferred_element_type=jnp.float32
        ).astype(jnp.bfloat16)
        part = part * jnp.bfloat16(head_dim ** (-0.5))
        query2[p, 0:rows] = jnp.where(first, part, jnp.zeros_like(part))
        query2[p, rows : 2 * rows] = jnp.where(first, jnp.zeros_like(part), part)

    def absorb(index):
        normed = normalize(shards[index].astype(jnp.float32), gain_ref[...]).astype(jnp.bfloat16)
        block = min(256, width)
        for c in range(2 * width // block):
            kv[:, c * block : (c + 1) * block] = jnp.dot(
                normed,
                win[:, width + c * block : width + (c + 1) * block],
                preferred_element_type=jnp.float32,
            ).astype(jnp.bfloat16)
        for p in range(pairs):
            keys = kv[:, p * pair : (p + 1) * pair]
            values = kv[:, width + p * pair : width + (p + 1) * pair]
            scores = lax.dot_general(
                query2[p], keys, (((1,), (1,)), ((), ())), preferred_element_type=jnp.float32
            )
            old = top[p][:, 0:1]
            new = jnp.maximum(old, jnp.max(scores, -1, keepdims=True))
            scale = jnp.exp(old - new)
            weights = jnp.exp(scores - new)
            total[p] = jnp.broadcast_to(
                total[p][:, 0:1] * scale + jnp.sum(weights, -1, keepdims=True), total.shape[1:]
            )
            top[p] = jnp.broadcast_to(new, top.shape[1:])
            acc[p] = acc[p] * scale + jnp.dot(
                weights.astype(jnp.bfloat16), values, preferred_element_type=jnp.float32
            )

    def step(distance, carry):
        low, high = me - distance, me + distance

        @pl.when((distance > 0) & (low >= 0))
        def _():
            to_left(shards.at[low], low).wait_recv()

            @pl.when(has_right)
            def _():
                to_right(shards.at[low], low).start()

        @pl.when((distance > 0) & (high < ranks))
        def _():
            to_right(shards.at[high], high).wait_recv()

            @pl.when(has_left)
            def _():
                to_left(shards.at[high], high).start()

        def side(which, inner):
            index = jnp.where(which == 0, low, high)

            @pl.when((index >= 0) & (index < ranks) & ((distance > 0) | (which == 0)))
            def _():
                absorb(index)

            return inner

        lax.fori_loop(0, 2, side, 0)
        return carry

    lax.fori_loop(0, ranks, step, 0)
    for p in range(pairs):
        even = acc[p, 0:rows] / total[p, 0:rows]
        odd = acc[p, rows : 2 * rows] / total[p, rows : 2 * rows]
        context[:, p * pair : (p + 1) * pair] = jnp.where(first, even, odd).astype(jnp.bfloat16)
    load_out.wait()
    hidden = tok_ref[...].astype(jnp.float32) + jnp.dot(
        context[...], wout[...], preferred_element_type=jnp.float32
    )
    hidden_buf[...] = hidden
    normed2_buf[...] = normalize(hidden, gain2_ref[...]).astype(jnp.bfloat16)

    def send(other_group, other_rank):
        return pltpu.make_async_remote_copy(
            src_ref=rows_buf.at[other_rank, other_group],
            dst_ref=arrived.at[me, group],
            send_sem=out_sem.at[other_rank, other_group],
            recv_sem=in_sem.at[me, group],
            device_id=place(other_group, other_rank),
            device_id_type=MESH,
        )

    def receive(other_group, other_rank):
        return pltpu.make_async_remote_copy(
            src_ref=rows_buf.at[me, group],
            dst_ref=arrived.at[other_rank, other_group],
            send_sem=out_sem.at[other_rank, other_group],
            recv_sem=in_sem.at[other_rank, other_group],
            device_id=place(other_group, other_rank),
            device_id_type=MESH,
        )

    def reply(other_group, other_rank):
        return pltpu.make_async_remote_copy(
            src_ref=result.at[other_rank, other_group],
            dst_ref=back.at[me, group],
            send_sem=reply_sem.at[other_rank, other_group],
            recv_sem=back_sem.at[me, group],
            device_id=place(other_group, other_rank),
            device_id_type=MESH,
        )

    def returned(other_group, other_rank):
        return pltpu.make_async_remote_copy(
            src_ref=result.at[other_rank, other_group],
            dst_ref=back.at[other_rank, other_group],
            send_sem=reply_sem.at[other_rank, other_group],
            recv_sem=back_sem.at[other_rank, other_group],
            device_id=place(other_group, other_rank),
            device_id_type=MESH,
        )

    def over_groups(rank, act):
        def one(offset, carry):
            other_group = (group + offset) % groups

            @pl.when((offset > 0) | (rank != me))
            def _():
                act(other_group, rank)

            return carry

        lax.fori_loop(0, groups, one, 0)

    def farthest_first(act):
        def one(step, carry):
            place_in_line = 2 * ranks - 2 - step
            distance = (place_in_line + 1) // 2
            rank = jnp.where(place_in_line % 2 == 1, me - distance, me + distance)

            @pl.when((rank >= 0) & (rank < ranks))
            def _():
                act(rank)

            return carry

        lax.fori_loop(0, 2 * ranks - 1, one, 0)

    def middle_first(act):
        def one(step, carry):
            distance = step // 2
            low = (ranks - 1) // 2
            near = jnp.where(step % 2 == 0, low - distance, low + 1 + distance)
            rank = jnp.where(2 * me >= ranks, ranks - 1 - near, near)

            @pl.when((rank >= 0) & (rank < ranks))
            def _():
                act(rank)

            return carry

        lax.fori_loop(0, ranks + 1, one, 0)

    slots = groups * most

    def label(rank, shape, dim):
        column = lax.broadcasted_iota(jnp.int32, shape, dim).astype(jnp.float32)
        block = jnp.floor((column + 0.5) * (1.0 / most))
        return (block * ranks + rank.astype(jnp.float32)) * most + (column - block * most)

    def scatter(rank):
        pick = (label(rank, (slots, rows), 0) == slot_row).astype(jnp.float32).astype(jnp.bfloat16)
        rows_buf[rank] = (
            jnp.dot(pick, normed2_buf[...], preferred_element_type=jnp.float32)
            .astype(jnp.bfloat16)
            .reshape(groups, most, width)
        )
        over_groups(rank, lambda g, r: send(g, r).start())

    farthest_first(scatter)
    arrived[me, group] = rows_buf[me, group]
    logits = jnp.dot(normed2_buf[...], router_ref[...], preferred_element_type=jnp.float32)
    gate = jax.nn.sigmoid(jnp.sum(logits * chosen, 1, keepdims=True))
    load1.wait()
    load2.wait()
    hidden_units = w1.shape[1]
    block = 256 if hidden_units % 256 == 0 else hidden_units
    out_block = 256 if width % 256 == 0 else width

    def work(rank):
        over_groups(rank, lambda g, r: receive(g, r).wait_recv())
        batch = arrived[rank].reshape(slots, width)
        for c in range(0, hidden_units, block):
            inner[:, c : c + block] = jax.nn.relu(
                jnp.dot(batch, w1[:, c : c + block], preferred_element_type=jnp.float32)
            ).astype(jnp.bfloat16)
        for c in range(0, width, out_block):
            result[rank, :, :, c : c + out_block] = (
                jnp.dot(inner[...], w2[:, c : c + out_block], preferred_element_type=jnp.float32)
                .astype(jnp.bfloat16)
                .reshape(groups, most, out_block)
            )
        over_groups(rank, lambda g, r: reply(g, r).start())

    middle_first(work)
    back[me, group] = result[me, group]
    combined[...] = jnp.zeros(combined.shape, jnp.float32)

    def gather(rank):
        over_groups(rank, lambda g, r: returned(g, r).wait_recv())
        pick = (label(rank, (rows, slots), 1) == slot_column).astype(jnp.float32).astype(jnp.bfloat16)
        combined[...] += jnp.dot(
            pick, back[rank].reshape(slots, width), preferred_element_type=jnp.float32
        )

    middle_first(gather)
    out_ref[...] = (hidden_buf[...] + gate * combined[...]).astype(jnp.bfloat16)
    farthest_first(lambda rank: over_groups(rank, lambda g, r: send(g, r).wait_send()))
    farthest_first(lambda rank: over_groups(rank, lambda g, r: reply(g, r).wait_send()))

    def drain(index, carry):
        @pl.when(has_right & (index <= me))
        def _():
            to_right(shards.at[index], index).wait_send()

        @pl.when(has_left & (index >= me))
        def _():
            to_left(shards.at[index], index).wait_send()

        return carry

    lax.fori_loop(0, ranks, drain, 0)


def layer(tokens, expert_ids, attn_in, attn_out, gain_attn, gain_expert, router, w1, w2):
    rows, width = tokens.shape
    sizes = tuple(lax.axis_size(name) for name in AXES)
    groups, ranks = sizes[0] * sizes[1], sizes[2]
    devices = groups * ranks
    most = max(2, 2 * rows // devices)
    head_dim = width // HEADS
    pair = 2 * head_dim
    pairs = width // pair
    vmem = pl.BlockSpec(memory_space=pltpu.VMEM)
    hbm = pl.BlockSpec(memory_space=pl.ANY)
    blocks = pltpu.VMEM((ranks, groups, most, width), jnp.bfloat16)
    per_device = pltpu.SemaphoreType.DMA((ranks, groups))
    return pl.pallas_call(
        functools.partial(layer_kernel, sizes, head_dim),
        out_shape=jax.ShapeDtypeStruct((rows, width), jnp.bfloat16),
        in_specs=[vmem, vmem, vmem, hbm, hbm, vmem, vmem, vmem, hbm, hbm],
        out_specs=vmem,
        scratch_shapes=[
            pltpu.VMEM((ranks, rows, width), jnp.bfloat16),
            pltpu.VMEM(attn_in.shape, jnp.bfloat16),
            pltpu.VMEM(attn_out.shape, jnp.bfloat16),
            pltpu.VMEM((pairs, 2 * rows, pair), jnp.bfloat16),
            pltpu.VMEM((rows, 2 * width), jnp.bfloat16),
            pltpu.VMEM((pairs, 2 * rows, pair), jnp.float32),
            pltpu.VMEM((pairs, 2 * rows, pair), jnp.float32),
            pltpu.VMEM((pairs, 2 * rows, pair), jnp.float32),
            pltpu.VMEM((rows, width), jnp.bfloat16),
            blocks,
            blocks,
            blocks,
            blocks,
            pltpu.VMEM((groups * most, w1.shape[1]), jnp.bfloat16),
            pltpu.VMEM(w1.shape, jnp.bfloat16),
            pltpu.VMEM(w2.shape, jnp.bfloat16),
            pltpu.VMEM((rows, width), jnp.float32),
            pltpu.VMEM((rows, width), jnp.bfloat16),
            pltpu.VMEM((rows, width), jnp.float32),
            pltpu.SemaphoreType.DMA((4,)),
            pltpu.SemaphoreType.DMA((ranks,)),
            pltpu.SemaphoreType.DMA((ranks,)),
            pltpu.SemaphoreType.DMA((ranks,)),
            per_device,
            per_device,
            per_device,
            per_device,
        ],
        compiler_params=pltpu.CompilerParams(
            collective_id=0, has_side_effects=True, vmem_limit_bytes=VMEM_LIMIT
        ),
    )(
        tokens,
        expert_ids,
        expert_ids.reshape(1, rows),
        attn_in,
        attn_out,
        gain_attn[None, :],
        gain_expert[None, :],
        router,
        w1,
        w2,
    )


def body(
    tokens, expert_ids, attn_in, attn_out, gain_attn, gain_expert, router, expert_in, expert_out
):
    return layer(
        tokens,
        expert_ids,
        attn_in,
        attn_out,
        gain_attn,
        gain_expert,
        router,
        expert_in[0],
        expert_out[0],
    )


def solution(mesh):
    return jax.shard_map(
        body,
        mesh=mesh,
        in_specs=(P(AXES, None), P(AXES, None), P(), P(), P(), P(), P(), P(AXES, None, None), P(AXES, None, None)),
        out_specs=P(AXES, None),
        check_vma=False,
    )
```

time: 125 us -> 119 us (0.952)
  matrix products: 6.47 us -> 0 us
  local copies, waits for them, and re-layouts: 0.2 us -> 5.02 us
  other arithmetic: 2.83 us -> 0 us
    dot_general x3 -> x0, matrix products: 6.47 us -> none  [the longest x1 2.64 us: body(): jnp.einsum('ts,td->sd', route, normed2, preferred_element_type=jnp.float32)]
    unnamed x6 -> x3, local copies, waits for them, and re-layouts: 0.01 us -> 5.02 us
    pallas_call x2 -> x1, Pallas kernels: 115 us -> 114 us  [layer(): pl.pallas_call(functools.partial(layer_kernel, sizes, head_dim), out_shap...]
where the time goes in v2:
time: 119 us
  Pallas kernels  114 us (96%)
  local copies, waits for them, and re-layouts  5.02 us (4%)
    pallas_call x1, Pallas kernels, layer(): pl.pallas_call(functools.partial(layer_kernel, sizes, head_dim), out_shap...  114 us
    unnamed x3, local copies, waits for them, and re-layouts  5.02 us

profile of v2, /device:TPU:1, one launch (start us, length us, event | category | flops | bytes accessed | tf_op | source)
XLA Modules:
  0.0 118.6 jit_solution(1328530339215786315)
XLA Ops:
  0.0 1.5 %copy.10.ids_ref = s32[256,1]{1,0:T(8,128)} copy(s32[256,1]{0,1:T(1,128)} %param.10) | data formatting | bytes 2048 | tf_op args[1]
  1.5 1.7 %copy.11.router_ref = bf16[1024,32]{1,0:T(8,128)(2,1)} copy(bf16[1024,32]{0,1:T(8,128)(2,1)} %param.15) | data formatting | bytes 131072 | tf_op args[6]
  3.1 113.5 %shard_map.91 = bf16[256,1024]{1,0:T(8,128)(2,1)} custom-call(bf16[256,1024]{1,0:T(8,128)(2,1)} %tok_ref.1, s32[256,1]{1,0:T(8,128)} %copy.10.ids_ref, s32[1,256]{1,0:T(1,128)} %bitcast.9, bf16[1024,3072]{1,0:T(8,128)(2,1)} %win_hbm.1, bf16[1024,1024]{1,0:T(8,128)(2,1)} %wout_hbm.1, f32[1,1024]{1,0:T(1,128)} %bitcast.7, f32[1,1024]{1,0:T(1,128)} %bitcast.8, ...), custom_call_target="tpu_custom_call" | custom-call | tf_op jit(solution)/shard_map/pallas_call | solution.py:393
  116.7 1.9 %copy.13 = bf16[256,1024]{1,0:T(8,128)(2,1)} copy(bf16[256,1024]{1,0:T(8,128)(2,1)} %shard_map.91) | data formatting | bytes 1048576

commit v3 on v2

--- a/solution.py
+++ b/solution.py
@@ -21,7 +21,6 @@
     sizes,
     head_dim,
     tok_ref,
-    ids_ref,
     ids_row_ref,
     win_hbm,
     wout_hbm,
@@ -124,16 +123,16 @@
 
     shards[me] = tok_ref[...]
     experts = devices
-    ids = ids_ref[...].astype(jnp.float32)
     ids_row = ids_row_ref[...].astype(jnp.float32)
-    chosen = (
-        lax.broadcasted_iota(jnp.int32, (rows, experts), 1).astype(jnp.float32) == ids
-    ).astype(jnp.float32)
     chosen_row = (
         lax.broadcasted_iota(jnp.int32, (experts, rows), 0).astype(jnp.float32) == ids_row
     ).astype(jnp.float32)
     down = lax.broadcasted_iota(jnp.int32, (rows, rows), 0)
     across = lax.broadcasted_iota(jnp.int32, (rows, rows), 1)
+    ids = jnp.sum(jnp.where(down == across, ids_row, 0.0), 1, keepdims=True)
+    chosen = (
+        lax.broadcasted_iota(jnp.int32, (rows, experts), 1).astype(jnp.float32) == ids
+    ).astype(jnp.float32)
     below = (across < down).astype(jnp.float32).astype(jnp.bfloat16)
     above = (down < across).astype(jnp.float32).astype(jnp.bfloat16)
     earlier = jnp.dot(below, chosen.astype(jnp.bfloat16), preferred_element_type=jnp.float32)
@@ -158,6 +157,7 @@
     def absorb(index):
         normed = normalize(shards[index].astype(jnp.float32), gain_ref[...]).astype(jnp.bfloat16)
         block = min(256, width)
+        ones = jnp.ones((rows, pair), jnp.bfloat16)
         for c in range(2 * width // block):
             kv[:, c * block : (c + 1) * block] = jnp.dot(
                 normed,
@@ -170,17 +170,19 @@
             scores = lax.dot_general(
                 query2[p], keys, (((1,), (1,)), ((), ())), preferred_element_type=jnp.float32
             )
-            old = top[p][:, 0:1]
+            old = top[p]
             new = jnp.maximum(old, jnp.max(scores, -1, keepdims=True))
             scale = jnp.exp(old - new)
-            weights = jnp.exp(scores - new)
-            total[p] = jnp.broadcast_to(
-                total[p][:, 0:1] * scale + jnp.sum(weights, -1, keepdims=True), total.shape[1:]
+            spread = jnp.concatenate([new] * (rows // pair), 1) if rows % pair == 0 else new[:, 0:1]
+            weights = jnp.exp(scores - spread).astype(jnp.bfloat16)
+            update = jnp.dot(
+                weights,
+                jnp.concatenate([values, ones], 1),
+                preferred_element_type=jnp.float32,
             )
-            top[p] = jnp.broadcast_to(new, top.shape[1:])
-            acc[p] = acc[p] * scale + jnp.dot(
-                weights.astype(jnp.bfloat16), values, preferred_element_type=jnp.float32
-            )
+            top[p] = new
+            acc[p] = acc[p] * scale + update[:, 0:pair]
+            total[p] = total[p] * scale + update[:, pair : 2 * pair]
 
     def step(distance, carry):
         low, high = me - distance, me + distance
@@ -277,19 +279,14 @@
 
         lax.fori_loop(0, groups, one, 0)
 
-    def farthest_first(act):
+    def across_first(act):
         def one(step, carry):
-            place_in_line = 2 * ranks - 2 - step
-            distance = (place_in_line + 1) // 2
-            rank = jnp.where(place_in_line % 2 == 1, me - distance, me + distance)
-
-            @pl.when((rank >= 0) & (rank < ranks))
-            def _():
-                act(rank)
-
+            half = ranks // 2
+            far = jnp.where(step < ranks - half, half + step, ranks - 1 - step)
+            act(jnp.where(2 * me >= ranks, ranks - 1 - far, far))
             return carry
 
-        lax.fori_loop(0, 2 * ranks - 1, one, 0)
+        lax.fori_loop(0, ranks, one, 0)
 
     def middle_first(act):
         def one(step, carry):
@@ -322,9 +319,14 @@
         )
         over_groups(rank, lambda g, r: send(g, r).start())
 
-    farthest_first(scatter)
+    across_first(scatter)
     arrived[me, group] = rows_buf[me, group]
-    logits = jnp.dot(normed2_buf[...], router_ref[...], preferred_element_type=jnp.float32)
+    logits = lax.dot_general(
+        normed2_buf[...],
+        router_ref[...],
+        (((1,), (1,)), ((), ())),
+        preferred_element_type=jnp.float32,
+    )
     gate = jax.nn.sigmoid(jnp.sum(logits * chosen, 1, keepdims=True))
     load1.wait()
     load2.wait()
@@ -360,8 +362,8 @@
 
     middle_first(gather)
     out_ref[...] = (hidden_buf[...] + gate * combined[...]).astype(jnp.bfloat16)
-    farthest_first(lambda rank: over_groups(rank, lambda g, r: send(g, r).wait_send()))
-    farthest_first(lambda rank: over_groups(rank, lambda g, r: reply(g, r).wait_send()))
+    across_first(lambda rank: over_groups(rank, lambda g, r: send(g, r).wait_send()))
+    across_first(lambda rank: over_groups(rank, lambda g, r: reply(g, r).wait_send()))
 
     def drain(index, carry):
         @pl.when(has_right & (index <= me))
@@ -393,7 +395,7 @@
     return pl.pallas_call(
         functools.partial(layer_kernel, sizes, head_dim),
         out_shape=jax.ShapeDtypeStruct((rows, width), jnp.bfloat16),
-        in_specs=[vmem, vmem, vmem, hbm, hbm, vmem, vmem, vmem, hbm, hbm],
+        in_specs=[vmem, vmem, hbm, hbm, vmem, vmem, vmem, hbm, hbm],
         out_specs=vmem,
         scratch_shapes=[
             pltpu.VMEM((ranks, rows, width), jnp.bfloat16),
@@ -429,13 +431,12 @@
         ),
     )(
         tokens,
-        expert_ids,
         expert_ids.reshape(1, rows),
         attn_in,
         attn_out,
         gain_attn[None, :],
         gain_expert[None, :],
-        router,
+        router.T,
         w1,
         w2,
     )

time: 119 us -> 101 us (0.85)
  Pallas kernels: 114 us -> 98.5 us
  local copies, waits for them, and re-layouts: 5.02 us -> 1.87 us
    pallas_call x1, Pallas kernels: 114 us -> 98.5 us  [layer(): pl.pallas_call(functools.partial(layer_kernel, sizes, head_dim), out_shap...]
    unnamed x3 -> x1, local copies, waits for them, and re-layouts: 5.02 us -> 1.87 us
where the time goes in v3:
time: 101 us; the launch traced here: 100 us
  Pallas kernels  98.5 us (98%)
  local copies, waits for them, and re-layouts  1.87 us (2%)
    pallas_call x1, Pallas kernels, layer(): pl.pallas_call(functools.partial(layer_kernel, sizes, head_dim), out_shap...  98.5 us

profile of v3, /device:TPU:1, one launch (start us, length us, event | category | flops | bytes accessed | tf_op | source)
XLA Modules:
  0.0 100.4 jit_solution(3986638832981897631)
XLA Ops:
  0.0 98.5 %shard_map.91 = bf16[256,1024]{1,0:T(8,128)(2,1)} custom-call(bf16[256,1024]{1,0:T(8,128)(2,1)} %tok_ref.1, s32[1,256]{1,0:T(1,128)} %bitcast.11, bf16[1024,3072]{1,0:T(8,128)(2,1)} %win_hbm.1, bf16[1024,1024]{1,0:T(8,128)(2,1)} %wout_hbm.1, f32[1,1024]{1,0:T(1,128)} %bitcast.9, f32[1,1024]{1,0:T(1,128)} %bitcast.10, bf16[32,1024]{1,0:T(8,128)(2,1)} %bitcast.8, ...), custom_call_target="tpu_custom_call" | custom-call | tf_op jit(solution)/shard_map/pallas_call | solution.py:395
  98.5 1.9 %copy.11 = bf16[256,1024]{1,0:T(8,128)(2,1)} copy(bf16[256,1024]{1,0:T(8,128)(2,1)} %shard_map.91) | data formatting | bytes 1048576
